TPU v7x, 32 devices: a whole 2x2x4 slice. The times are simulated.
32 devices in a mesh: row: 8 (over z, y), col: 4 (over x, core).
Axes of the slice: x: 2, y: 2, z: 4, core: 2. Of those that a mesh axis runs over, the one named last changes fastest.
Arguments:
- rhs: float32 [32768, 256], P(('row', 'col')), may hold values from -6 to 6
- local_mat: bfloat16 [32768, 1024], P(('row', 'col')), may hold values from -1 to 5
- local_inv: bfloat16 [32768, 1024], P(('row', 'col')), may hold values from -1 to 1
- basis_t: bfloat16 [3072, 1024], P(('row', 'col')), may hold values from -0.1875 to 0.1875
- coarse_inv: bfloat16 [3072, 3072], P('col', 'row'), may hold values from -0.109375 to 0.109375
- couple: float32 [32, 4, 128], P(('row', 'col')), may hold values from 0.5 to 2
- margin_rows: int32 [32, 4, 128], P(('row', 'col')), may hold values from 0 to 1023, as said below
Outputs:
- solution: float32 [32768, 256], P(('row', 'col'))
- residual: float32 [32768, 256], P(('row', 'col'))
Inputs may be any that keep to these rules, and one draw needn't show every extreme that they name: `margin_rows`: within each subdomain the 512 listed rows are all different.
All inputs are finite; a program needn't handle non-finite values.
Results may differ from a plain program's by a relative error of at most 0.024.
Values may be sent and summed in bfloat16 or wider, within the bound.
No kernel may reach another device: no remote copies, remote signals or barrier semaphores. Data moves between devices by JAX's collectives and lax.ppermute only.
A program may use at most 64 MiB of HBM per device.

v0:
```python
import jax
import jax.numpy as jnp
from jax import lax
from jax.sharding import PartitionSpec as P

STEPS = 2


def padded(cells, sides, width):
    for axis, dim in sides:
        count = lax.axis_size(axis)
        ends = count - 1
        head = lax.slice_in_dim(cells, 0, width, axis=dim)
        tail = lax.slice_in_dim(cells, cells.shape[dim] - width, cells.shape[dim], axis=dim)
        cells = jnp.concatenate(
            [
                lax.ppermute(tail, axis, [(i, (i + 1) % count) for i in range(ends)]),
                cells,
                lax.ppermute(head, axis, [((i + 1) % count, i) for i in range(ends)]),
            ],
            axis=dim,
        )
    return cells


def per_device(rhs, local_mat, local_inv, basis_t, coarse_inv, couple, margin_rows):
    face_index = margin_rows[0]
    flat_rows = face_index.reshape(-1)
    weights = couple[0]
    columns = rhs.shape[1]

    def neighbour_faces(vector_b):
        face_vals = vector_b[face_index]
        north_south = padded(face_vals[0:2], (("row", 0),), 1)
        west_east = padded(face_vals[2:4], (("col", 0),), 1)
        received = jnp.stack([north_south[0], north_south[3], west_east[0], west_east[3]])
        return received

    def apply_operator(vector):
        vector_b = vector.astype(jnp.bfloat16)
        received = neighbour_faces(vector_b)
        coupling_terms = (weights[:, :, None] * received.astype(jnp.float32)).reshape(-1, columns)
        coupled = jnp.zeros(vector.shape, jnp.float32).at[flat_rows].add(coupling_terms)
        return jnp.dot(local_mat, vector_b, preferred_element_type=jnp.float32) - coupled

    solution = jnp.zeros(rhs.shape, jnp.float32)
    residual = rhs
    for sweep in range(STEPS):
        if sweep > 0:
            residual = rhs - apply_operator(solution)
        rounded = residual.astype(jnp.bfloat16)
        restricted = jnp.dot(basis_t, rounded, preferred_element_type=jnp.float32).astype(
            jnp.bfloat16
        )
        block_rows = restricted.shape[0]
        partial_sum = jnp.dot(
            coarse_inv,
            lax.all_gather(restricted, "col", axis=0, tiled=True),
            preferred_element_type=jnp.float32,
        )
        summed = lax.psum(partial_sum, "row")
        coarse_part = lax.dynamic_slice_in_dim(
            summed, lax.axis_index("row") * block_rows, block_rows, 0
        )
        coarse_b = coarse_part.astype(jnp.bfloat16)
        solution = solution + lax.dot_general(
            basis_t, coarse_b, (((0,), (0,)), ((), ())), preferred_element_type=jnp.float32
        )
        residual = rhs - apply_operator(solution)
        solution = solution + jnp.dot(
            local_inv, residual.astype(jnp.bfloat16), preferred_element_type=jnp.float32
        )
    residual = rhs - apply_operator(solution)
    return (solution, residual)


def solution(mesh):
    placed = (
        P(("row", "col"), None),
        P(("row", "col"), None),
        P(("row", "col"), None),
        P(("row", "col"), None),
        P("col", "row"),
        P(("row", "col"), None, None),
        P(("row", "col"), None, None),
    )
    return jax.shard_map(
        per_device,
        mesh=mesh,
        in_specs=placed,
        out_specs=(P(("row", "col"), None), P(("row", "col"), None)),
        check_vma=False,
    )
```

profile of v0, /device:TPU:9, one launch (start us, length us, event | category | flops | bytes accessed | tf_op | source)
XLA Modules:
  0.0 242.6 jit_solution(8589869174017089495)
XLA Ops:
  3.1 6.1 %all_gather.6 = bf16[384,256]{1,0:T(8,128)(2,1)S(1)} all-gather(bf16[96,256]{1,0:T(8,128)(2,1)S(1)} %convolution_convert_fusion), channel_id=1, replica_groups=mesh['row'=8,'col'=4] {'col'}, dimensions={0}, use_global_device_ids=true | all-gather | bytes 245760 | tf_op jit(solution)/shard_map/all_gather | solution.py:58
  10.7 40.2 %all-reduce.2 = bf16[768,256]{0,1:T(8,128)(2,1)} all-reduce(f32[768,256]{0,1:T(8,128)S(1)} %convolution_bitcast_fusion.5), channel_id=1, replica_groups=mesh['row'=8,'col'=4] {'row'}, use_global_device_ids=true, to_apply=%region_0.0 | all-reduce | flops 196608 | bytes 1179648 | tf_op jit(solution)/shard_map/psum | solution.py:61
  57.9 8.7 %collective-permute-start.2 = (bf16[1,128,256]{2,1,0:T(8,128)(2,1)}, bf16[1,128,256]{2,1,0:T(8,128)(2,1)}, u32[]{:S(2)}, u32[]{:S(2)}) collective-permute-start(bf16[1,128,256]{2,1,0:T(8,128)(2,1)} %get-tuple-element.21), channel_id=1, source_target_pairs={{0,1},{1,2},{2,3},{4,5},{5,6},{6,7},{8,9},{9,10},{10,11},{12,13},{... | collective-permute-start | bytes 196616 | tf_op jit(solution)/shard_map/ppermute | solution.py:17
  66.6 3.3 %collective-permute-start.1 = (bf16[1,128,256]{2,1,0:T(8,128)(2,1)S(1)}, bf16[1,128,256]{2,1,0:T(8,128)(2,1)}, u32[]{:S(2)}, u32[]{:S(2)}) collective-permute-start(bf16[1,128,256]{2,1,0:T(8,128)(2,1)S(1)} %get-tuple-element.22), channel_id=1, source_target_pairs={{4,0},{8,4},{12,8},{16,12},{20,16},{24,20},{28,24},{5,1},{9,5},{13... | collective-permute-start | bytes 196616 | tf_op jit(solution)/shard_map/ppermute | solution.py:19
  77.3 4.8 %scatter_custom_fusion = f32[1024,256]{1,0:T(8,128)} fusion(s32[512]{0:T(512)S(1)} %bitcast.127, bf16[512,256]{1,0:T(8,128)(2,1)} %bitcast.119, f32[]{:T(128)} %constant.4.clone.1, f32[512]{0:T(512)S(1)} %bitcast.122), kind=kCustom, calls=%fused_computation.40 | custom fusion | flops 393216 | bytes 1312772 | tf_op jit(solution)/shard_map/scatter-add | solution.py:43
  84.6 4.8 %convolution_add_fusion.2 = f32[256,1024]{1,0:T(8,128)} fusion(f32[256,1024]{1,0:T(8,128)} %copy-done.2, bf16[1024,1024]{1,0:T(8,128)(2,1)} %param.9, f32[1024,256]{0,1:T(8,128)S(1)} %copy.33, f32[1024,256]{0,1:T(8,128)} %copy.32, bf16[1024,1024]{1,0:T(8,128)(2,1)S(1)} %copy-done), kind=kOutput, calls=%fused_computation.23 | convolution fusion | flops 1075052544 | bytes 8388608 | tf_op jit(solution)/shard_map/dot_general | solution.py:70
  93.5 3.3 %gather_fusion.1 = bf16[512,256]{1,0:T(8,128)(2,1)} fusion(bf16[1024,256]{1,0:T(8,128)(2,1)} %copy.34, s32[1024]{0:T(1024)S(1)} %pad_clamp_fusion), kind=kCustom, calls=%fused_computation.1 | custom fusion | bytes 526336 | tf_op jit(solution)/shard_map/gather | solution.py:33
  101.8 4.2 %collective-permute-start.5 = (bf16[1,128,256]{2,1,0:T(8,128)(2,1)S(1)}, bf16[1,128,256]{2,1,0:T(8,128)(2,1)S(1)}, u32[]{:S(2)}, u32[]{:S(2)}) collective-permute-start(bf16[1,128,256]{2,1,0:T(8,128)(2,1)S(1)} %get-tuple-element.18), channel_id=1, source_target_pairs={{4,0},{8,4},{12,8},{16,12},{20,16},{24,20},{28,24},{5,1},{9,5},{13... | collective-permute-start | bytes 196616 | tf_op jit(solution)/shard_map/ppermute | solution.py:19
  106.0 2.6 %collective-permute-start.7 = (bf16[1,128,256]{2,1,0:T(8,128)(2,1)S(1)}, bf16[1,128,256]{2,1,0:T(8,128)(2,1)S(1)}, u32[]{:S(2)}, u32[]{:S(2)}) collective-permute-start(bf16[1,128,256]{2,1,0:T(8,128)(2,1)S(1)} %get-tuple-element.19), channel_id=1, source_target_pairs={{1,0},{2,1},{3,2},{5,4},{6,5},{7,6},{9,8},{10,9},{11,10},{13,12},{... | collective-permute-start | bytes 196616 | tf_op jit(solution)/shard_map/ppermute | solution.py:19
  108.6 3.0 %collective-permute-done.7 = bf16[1,128,256]{2,1,0:T(8,128)(2,1)S(1)} collective-permute-done((bf16[1,128,256]{2,1,0:T(8,128)(2,1)S(1)}, bf16[1,128,256]{2,1,0:T(8,128)(2,1)S(1)}, u32[]{:S(2)}, u32[]{:S(2)}) %collective-permute-start.7) | collective-permute-done | bytes 65568 | tf_op jit(solution)/shard_map/ppermute | solution.py:19
  112.3 4.8 %scatter_custom_fusion.1 = f32[1024,256]{1,0:T(8,128)} fusion(s32[512]{0:T(512)S(1)} %bitcast.128, bf16[512,256]{1,0:T(8,128)(2,1)} %bitcast.120, f32[]{:T(128)} %constant.4.clone.1, f32[512]{0:T(512)S(1)} %bitcast.123), kind=kCustom, calls=%fused_computation.38 | custom fusion | flops 393216 | bytes 1312772 | tf_op jit(solution)/shard_map/scatter-add | solution.py:43
  122.2 4.4 %all_gather.7 = bf16[384,256]{1,0:T(8,128)(2,1)S(1)} all-gather(bf16[96,256]{1,0:T(8,128)(2,1)S(1)} %fusion.14), channel_id=1, replica_groups=mesh['row'=8,'col'=4] {'col'}, dimensions={0}, use_global_device_ids=true | all-gather | bytes 245760 | tf_op jit(solution)/shard_map/all_gather | solution.py:58
  129.0 39.4 %all-reduce.3 = bf16[768,256]{0,1:T(8,128)(2,1)} all-reduce(f32[768,256]{0,1:T(8,128)} %convolution_bitcast_fusion.4), channel_id=1, replica_groups=mesh['row'=8,'col'=4] {'row'}, use_global_device_ids=true, to_apply=%region_3.0 | all-reduce | flops 196608 | bytes 1179648 | tf_op jit(solution)/shard_map/psum | solution.py:61
  173.9 2.7 %gather_fusion.2 = bf16[512,256]{1,0:T(8,128)(2,1)S(1)} fusion(bf16[1024,256]{1,0:T(8,128)(2,1)} %copy.37, s32[1024]{0:T(1024)S(1)} %pad_clamp_fusion), kind=kCustom, calls=%fused_computation.2 | custom fusion | bytes 526336 | tf_op jit(solution)/shard_map/gather | solution.py:33
  178.6 8.4 %collective-permute-start.10 = (bf16[1,128,256]{2,1,0:T(8,128)(2,1)S(1)}, bf16[1,128,256]{2,1,0:T(8,128)(2,1)S(1)}, u32[]{:S(2)}, u32[]{:S(2)}) collective-permute-start(bf16[1,128,256]{2,1,0:T(8,128)(2,1)S(1)} %get-tuple-element.13), channel_id=1, source_target_pairs={{0,1},{1,2},{2,3},{4,5},{5,6},{6,7},{8,9},{9,10},{10,11},{12,13},{... | collective-permute-start | bytes 196616 | tf_op jit(solution)/shard_map/ppermute | solution.py:17
  187.0 4.5 %collective-permute-start.9 = (bf16[1,128,256]{2,1,0:T(8,128)(2,1)S(1)}, bf16[1,128,256]{2,1,0:T(8,128)(2,1)S(1)}, u32[]{:S(2)}, u32[]{:S(2)}) collective-permute-start(bf16[1,128,256]{2,1,0:T(8,128)(2,1)S(1)} %get-tuple-element.14), channel_id=1, source_target_pairs={{4,0},{8,4},{12,8},{16,12},{20,16},{24,20},{28,24},{5,1},{9,5},{13... | collective-permute-start | bytes 196616 | tf_op jit(solution)/shard_map/ppermute | solution.py:19
  193.5 3.6 %collective-permute-done.11 = bf16[1,128,256]{2,1,0:T(8,128)(2,1)S(1)} collective-permute-done((bf16[1,128,256]{2,1,0:T(8,128)(2,1)S(1)}, bf16[1,128,256]{2,1,0:T(8,128)(2,1)S(1)}, u32[]{:S(2)}, u32[]{:S(2)}) %collective-permute-start.11) | collective-permute-done | bytes 65568 | tf_op jit(solution)/shard_map/ppermute | solution.py:19
  197.2 4.4 %scatter_custom_fusion.2 = f32[1024,256]{1,0:T(8,128)} fusion(s32[512]{0:T(512)S(1)} %bitcast.129, bf16[512,256]{1,0:T(8,128)(2,1)S(1)} %bitcast.121, f32[]{:T(128)} %constant.4.clone.1, f32[512]{0:T(512)S(1)} %bitcast.124), kind=kCustom, calls=%fused_computation.36 | custom fusion | flops 393216 | bytes 1312772 | tf_op jit(solution)/shard_map/scatter-add | solution.py:43
  201.6 2.6 %copy.38 = f32[1024,256]{0,1:T(8,128)} copy(f32[1024,256]{1,0:T(8,128)} %scatter_custom_fusion.2) | data formatting | bytes 2097152 | tf_op jit(solution)/shard_map/scatter-add | solution.py:43
  204.2 5.0 %fusion.38 = (bf16[1024,256]{0,1:T(8,128)(2,1)}, f32[1024,256]{0,1:T(8,128)}) fusion(f32[256,1024]{1,0:T(8,128)} %copy-done.1, bf16[1024,1024]{1,0:T(8,128)(2,1)} %param.9, f32[1024,256]{0,1:T(8,128)S(1)} %copy.33, f32[1024,256]{0,1:T(8,128)} %copy.38, bf16[1024,1024]{1,0:T(8,128)(2,1)S(1)} %copy-done), kind=kOutput, calls=%fused_computation.85 | convolution fusion | flops 1075314688 | bytes 8912896 | tf_op jit(solution)/shard_map/dot_general | solution.py:70
  211.2 2.7 %gather_fusion.3 = bf16[512,256]{1,0:T(8,128)(2,1)S(1)} fusion(bf16[1024,256]{1,0:T(8,128)(2,1)} %copy.40, s32[1024]{0:T(1024)S(1)} %pad_clamp_fusion), kind=kCustom, calls=%fused_computation.3 | custom fusion | bytes 526336 | tf_op jit(solution)/shard_map/gather | solution.py:33
  218.3 4.5 %collective-permute-start.13 = (bf16[1,128,256]{2,1,0:T(8,128)(2,1)}, bf16[1,128,256]{2,1,0:T(8,128)(2,1)S(1)}, u32[]{:S(2)}, u32[]{:S(2)}) collective-permute-start(bf16[1,128,256]{2,1,0:T(8,128)(2,1)} %get-tuple-element.10), channel_id=1, source_target_pairs={{4,0},{8,4},{12,8},{16,12},{20,16},{24,20},{28,24},{5,1},{9,5},{13... | collective-permute-start | bytes 196616 | tf_op jit(solution)/shard_map/ppermute | solution.py:19
  230.0 4.4 %scatter_custom_fusion.3 = f32[1024,256]{1,0:T(8,128)} fusion(s32[512]{0:T(512)S(1)} %bitcast.130, bf16[512,256]{1,0:T(8,128)(2,1)S(1)} %bitcast.118, f32[]{:T(128)} %constant.4.clone.1, f32[512]{0:T(512)S(1)} %bitcast.125), kind=kCustom, calls=%fused_computation.34 | custom fusion | flops 393216 | bytes 1312772 | tf_op jit(solution)/shard_map/scatter-add | solution.py:43
  237.0 3.1 %fusion.7 = f32[1024,256]{0,1:T(8,128)} fusion(f32[1024,256]{0,1:T(8,128)S(1)} %copy.33, f32[1024,256]{0,1:T(8,128)} %copy.41, bf16[1024,256]{0,1:T(8,128)(2,1)} %get-tuple-element.24, bf16[1024,1024]{1,0:T(8,128)(2,1)S(1)} %copy-done), kind=kOutput, calls=%fused_computation.20 | convolution fusion | flops 537395200 | bytes 5767168 | tf_op jit(solution)/shard_map/dot_general | solution.py:44
  (70 shorter events, 66.1 us)
Async XLA Ops:
  0.6 84.0 %copy-start = (bf16[1024,1024]{1,0:T(8,128)(2,1)S(1)}, bf16[1024,1024]{1,0:T(8,128)(2,1)}, u32[]{:S(2)}) copy-start(bf16[1024,1024]{1,0:T(8,128)(2,1)} %param.8) | copy-start | bytes 6291460
  1.5 49.4 %copy-start.3 = (bf16[96,1024]{1,0:T(8,128)(2,1)S(1)}, bf16[96,1024]{1,0:T(8,128)(2,1)}, u32[]{:S(2)}) copy-start(bf16[96,1024]{1,0:T(8,128)(2,1)} %param.10) | copy-start | bytes 589828
  52.1 1.0 copy-start.2
  53.1 18.7 %copy-start.7 = (s32[1,4,128]{2,1,0:T(4,128)S(1)}, s32[1,4,128]{2,1,0:T(4,128)}, u32[]{:S(2)}) copy-start(s32[1,4,128]{2,1,0:T(4,128)} %param.13) | copy-start | bytes 6148
  55.3 21.9 %copy-start.6 = (f32[1,4,128]{2,1,0:T(4,128)S(1)}, f32[1,4,128]{2,1,0:T(4,128)}, u32[]{:S(2)}) copy-start(f32[1,4,128]{2,1,0:T(4,128)} %param.12) | copy-start | bytes 6148
  56.0 17.5 %collective-permute-start = (bf16[1,128,256]{2,1,0:T(8,128)(2,1)}, bf16[1,128,256]{2,1,0:T(8,128)(2,1)S(1)}, u32[]{:S(2)}, u32[]{:S(2)}) collective-permute-start(bf16[1,128,256]{2,1,0:T(8,128)(2,1)} %get-tuple-element.20), channel_id=1, source_target_pairs={{0,4},{4,8},{8,12},{12,16},{16,20},{20,24},{24,28},{1,5},{5,9},{9,... | collective-permute-start | bytes 196616 | tf_op jit(solution)/shard_map/ppermute | solution.py:17
  57.9 15.6 %collective-permute-start.2 = (bf16[1,128,256]{2,1,0:T(8,128)(2,1)}, bf16[1,128,256]{2,1,0:T(8,128)(2,1)}, u32[]{:S(2)}, u32[]{:S(2)}) collective-permute-start(bf16[1,128,256]{2,1,0:T(8,128)(2,1)} %get-tuple-element.21), channel_id=1, source_target_pairs={{0,1},{1,2},{2,3},{4,5},{5,6},{6,7},{8,9},{9,10},{10,11},{12,13},{... | collective-permute-start | bytes 196616 | tf_op jit(solution)/shard_map/ppermute | solution.py:17
  66.6 6.9 %collective-permute-start.1 = (bf16[1,128,256]{2,1,0:T(8,128)(2,1)S(1)}, bf16[1,128,256]{2,1,0:T(8,128)(2,1)}, u32[]{:S(2)}, u32[]{:S(2)}) collective-permute-start(bf16[1,128,256]{2,1,0:T(8,128)(2,1)S(1)} %get-tuple-element.22), channel_id=1, source_target_pairs={{4,0},{8,4},{12,8},{16,12},{20,16},{24,20},{28,24},{5,1},{9,5},{13... | collective-permute-start | bytes 196616 | tf_op jit(solution)/shard_map/ppermute | solution.py:19
  69.9 5.7 %collective-permute-start.3 = (bf16[1,128,256]{2,1,0:T(8,128)(2,1)S(1)}, bf16[1,128,256]{2,1,0:T(8,128)(2,1)}, u32[]{:S(2)}, u32[]{:S(2)}) collective-permute-start(bf16[1,128,256]{2,1,0:T(8,128)(2,1)S(1)} %get-tuple-element.23), channel_id=1, source_target_pairs={{1,0},{2,1},{3,2},{5,4},{6,5},{7,6},{9,8},{10,9},{11,10},{13,12},{... | collective-permute-start | bytes 196616 | tf_op jit(solution)/shard_map/ppermute | solution.py:19
  97.8 10.8 %collective-permute-start.4 = (bf16[1,128,256]{2,1,0:T(8,128)(2,1)S(1)}, bf16[1,128,256]{2,1,0:T(8,128)(2,1)S(1)}, u32[]{:S(2)}, u32[]{:S(2)}) collective-permute-start(bf16[1,128,256]{2,1,0:T(8,128)(2,1)S(1)} %get-tuple-element.16), channel_id=1, source_target_pairs={{0,4},{4,8},{8,12},{12,16},{16,20},{20,24},{24,28},{1,5},{5,9},{9,... | collective-permute-start | bytes 196616 | tf_op jit(solution)/shard_map/ppermute | solution.py:17
  99.7 8.9 %collective-permute-start.6 = (bf16[1,128,256]{2,1,0:T(8,128)(2,1)S(1)}, bf16[1,128,256]{2,1,0:T(8,128)(2,1)S(1)}, u32[]{:S(2)}, u32[]{:S(2)}) collective-permute-start(bf16[1,128,256]{2,1,0:T(8,128)(2,1)S(1)} %get-tuple-element.17), channel_id=1, source_target_pairs={{0,1},{1,2},{2,3},{4,5},{5,6},{6,7},{8,9},{9,10},{10,11},{12,13},{... | collective-permute-start | bytes 196616 | tf_op jit(solution)/shard_map/ppermute | solution.py:17
  101.8 6.8 %collective-permute-start.5 = (bf16[1,128,256]{2,1,0:T(8,128)(2,1)S(1)}, bf16[1,128,256]{2,1,0:T(8,128)(2,1)S(1)}, u32[]{:S(2)}, u32[]{:S(2)}) collective-permute-start(bf16[1,128,256]{2,1,0:T(8,128)(2,1)S(1)} %get-tuple-element.18), channel_id=1, source_target_pairs={{4,0},{8,4},{12,8},{16,12},{20,16},{24,20},{28,24},{5,1},{9,5},{13... | collective-permute-start | bytes 196616 | tf_op jit(solution)/shard_map/ppermute | solution.py:19
  106.0 5.6 %collective-permute-start.7 = (bf16[1,128,256]{2,1,0:T(8,128)(2,1)S(1)}, bf16[1,128,256]{2,1,0:T(8,128)(2,1)S(1)}, u32[]{:S(2)}, u32[]{:S(2)}) collective-permute-start(bf16[1,128,256]{2,1,0:T(8,128)(2,1)S(1)} %get-tuple-element.19), channel_id=1, source_target_pairs={{1,0},{2,1},{3,2},{5,4},{6,5},{7,6},{9,8},{10,9},{11,10},{13,12},{... | collective-permute-start | bytes 196616 | tf_op jit(solution)/shard_map/ppermute | solution.py:19
  170.0 1.0 copy-start.1
  176.6 16.8 %collective-permute-start.8 = (bf16[1,128,256]{2,1,0:T(8,128)(2,1)S(1)}, bf16[1,128,256]{2,1,0:T(8,128)(2,1)S(1)}, u32[]{:S(2)}, u32[]{:S(2)}) collective-permute-start(bf16[1,128,256]{2,1,0:T(8,128)(2,1)S(1)} %get-tuple-element.12), channel_id=1, source_target_pairs={{0,4},{4,8},{8,12},{12,16},{16,20},{20,24},{24,28},{1,5},{5,9},{9,... | collective-permute-start | bytes 196616 | tf_op jit(solution)/shard_map/ppermute | solution.py:17
  178.6 14.9 %collective-permute-start.10 = (bf16[1,128,256]{2,1,0:T(8,128)(2,1)S(1)}, bf16[1,128,256]{2,1,0:T(8,128)(2,1)S(1)}, u32[]{:S(2)}, u32[]{:S(2)}) collective-permute-start(bf16[1,128,256]{2,1,0:T(8,128)(2,1)S(1)} %get-tuple-element.13), channel_id=1, source_target_pairs={{0,1},{1,2},{2,3},{4,5},{5,6},{6,7},{8,9},{9,10},{10,11},{12,13},{... | collective-permute-start | bytes 196616 | tf_op jit(solution)/shard_map/ppermute | solution.py:17
  187.0 6.5 %collective-permute-start.9 = (bf16[1,128,256]{2,1,0:T(8,128)(2,1)S(1)}, bf16[1,128,256]{2,1,0:T(8,128)(2,1)S(1)}, u32[]{:S(2)}, u32[]{:S(2)}) collective-permute-start(bf16[1,128,256]{2,1,0:T(8,128)(2,1)S(1)} %get-tuple-element.14), channel_id=1, source_target_pairs={{4,0},{8,4},{12,8},{16,12},{20,16},{24,20},{28,24},{5,1},{9,5},{13... | collective-permute-start | bytes 196616 | tf_op jit(solution)/shard_map/ppermute | solution.py:19
  191.5 5.6 %collective-permute-start.11 = (bf16[1,128,256]{2,1,0:T(8,128)(2,1)S(1)}, bf16[1,128,256]{2,1,0:T(8,128)(2,1)S(1)}, u32[]{:S(2)}, u32[]{:S(2)}) collective-permute-start(bf16[1,128,256]{2,1,0:T(8,128)(2,1)S(1)} %get-tuple-element.15), channel_id=1, source_target_pairs={{1,0},{2,1},{3,2},{5,4},{6,5},{7,6},{9,8},{10,9},{11,10},{13,12},{... | collective-permute-start | bytes 196616 | tf_op jit(solution)/shard_map/ppermute | solution.py:19
  214.5 13.3 %collective-permute-start.12 = (bf16[1,128,256]{2,1,0:T(8,128)(2,1)}, bf16[1,128,256]{2,1,0:T(8,128)(2,1)S(1)}, u32[]{:S(2)}, u32[]{:S(2)}) collective-permute-start(bf16[1,128,256]{2,1,0:T(8,128)(2,1)} %get-tuple-element.8), channel_id=1, source_target_pairs={{0,4},{4,8},{8,12},{12,16},{16,20},{20,24},{24,28},{1,5},{5,9},{9,... | collective-permute-start | bytes 196616 | tf_op jit(solution)/shard_map/ppermute | solution.py:17
  216.4 11.4 %collective-permute-start.14 = (bf16[1,128,256]{2,1,0:T(8,128)(2,1)}, bf16[1,128,256]{2,1,0:T(8,128)(2,1)S(1)}, u32[]{:S(2)}, u32[]{:S(2)}) collective-permute-start(bf16[1,128,256]{2,1,0:T(8,128)(2,1)} %get-tuple-element.9), channel_id=1, source_target_pairs={{0,1},{1,2},{2,3},{4,5},{5,6},{6,7},{8,9},{9,10},{10,11},{12,13},{... | collective-permute-start | bytes 196616 | tf_op jit(solution)/shard_map/ppermute | solution.py:17
  218.3 9.5 %collective-permute-start.13 = (bf16[1,128,256]{2,1,0:T(8,128)(2,1)}, bf16[1,128,256]{2,1,0:T(8,128)(2,1)S(1)}, u32[]{:S(2)}, u32[]{:S(2)}) collective-permute-start(bf16[1,128,256]{2,1,0:T(8,128)(2,1)} %get-tuple-element.10), channel_id=1, source_target_pairs={{4,0},{8,4},{12,8},{16,12},{20,16},{24,20},{28,24},{5,1},{9,5},{13... | collective-permute-start | bytes 196616 | tf_op jit(solution)/shard_map/ppermute | solution.py:19
  222.8 6.2 %collective-permute-start.15 = (bf16[1,128,256]{2,1,0:T(8,128)(2,1)S(1)}, bf16[1,128,256]{2,1,0:T(8,128)(2,1)}, u32[]{:S(2)}, u32[]{:S(2)}) collective-permute-start(bf16[1,128,256]{2,1,0:T(8,128)(2,1)S(1)} %get-tuple-element.11), channel_id=1, source_target_pairs={{1,0},{2,1},{3,2},{5,4},{6,5},{7,6},{9,8},{10,9},{11,10},{13,12},{... | collective-permute-start | bytes 196616 | tf_op jit(solution)/shard_map/ppermute | solution.py:19
  227.8 0.6 copy-start.4
  228.5 0.6 copy-start.5
where the time goes:
time: 244 us; the launch traced here: 243 us
  blocking collectives  90.2 us (37%)
  starting transfers between devices  54.2 us (22%)
  local copies, waits for them, and re-layouts  39.2 us (16%)
  other arithmetic  25.7 us (11%)
  matrix products  23.6 us (10%)
  waiting for transfers between devices  8.78 us (4%)
    psum x2, blocking collectives, per_device(): summed = lax.psum(partial_sum, 'row')  79.6 us
    ppermute x8, starting transfers between devices, padded(): lax.ppermute(tail, axis, [(i, (i + 1) % count) for i in range(ends)])  28.7 us
    ppermute x8, starting transfers between devices, padded(): lax.ppermute(head, axis, [((i + 1) % count, i) for i in range(ends)])  25.5 us
    scatter-add x4, other arithmetic, apply_operator(): jnp.zeros(vector.shape, jnp.float32).at[flat_rows].add(coupling_terms)  18.5 us
    gather x4, local copies, waits for them, and re-layouts, neighbour_faces(): face_vals = vector_b[face_index]  10.6 us
    all_gather x2, blocking collectives, per_device(): lax.all_gather(restricted, 'col', axis=0, tiled=True)  10.6 us
    scatter-add x4, local copies, waits for them, and re-layouts, apply_operator(): jnp.zeros(vector.shape, jnp.float32).at[flat_rows].add(coupling_terms)  10.2 us
    unnamed x19, local copies, waits for them, and re-layouts  9.8 us
  transfers between devices with their start and end apart: 16, of which 3 were waited for; matrix products, arithmetic and copies ran while one was open for 2% of the time, Pallas kernels for 0%

commit v1 on v0

--- a/solution.py
+++ b/solution.py
@@ -4,6 +4,15 @@
 from jax.sharding import PartitionSpec as P
 
 STEPS = 2
+
+
+def sum_by_hops(shard, axis):
+    size = lax.axis_size(axis)
+    total, hop = (shard, 1)
+    while hop < size:
+        total = total + lax.ppermute(total, axis, [(i, i ^ hop) for i in range(size)])
+        hop = 2 * hop
+    return total
 
 
 def padded(cells, sides, width):
@@ -58,7 +67,7 @@
             lax.all_gather(restricted, "col", axis=0, tiled=True),
             preferred_element_type=jnp.float32,
         )
-        summed = lax.psum(partial_sum, "row")
+        summed = sum_by_hops(partial_sum, "row")
         coarse_part = lax.dynamic_slice_in_dim(
             summed, lax.axis_index("row") * block_rows, block_rows, 0
         )

time: 244 us -> 302 us (1.24)
  waiting for transfers between devices: 8.78 us -> 148 us
  blocking collectives: 90.2 us -> 10.6 us
    ppermute x0 -> x6, waiting for transfers between devices: none -> 139 us  [sum_by_hops(): lax.ppermute(total, axis, [(i, i ^ hop) for i in range(size)])]
    psum x2 -> x0, blocking collectives: 79.6 us -> none  [per_device(): summed = lax.psum(partial_sum, 'row')]
    ppermute x0 -> x6, starting transfers between devices: none -> 7.81 us  [sum_by_hops(): lax.ppermute(total, axis, [(i, i ^ hop) for i in range(size)])]
    ppermute x8, starting transfers between devices: 28.7 us -> 21.6 us  [padded(): lax.ppermute(tail, axis, [(i, (i + 1) % count) for i in range(ends)])]
    unnamed x19 -> x21, local copies, waits for them, and re-layouts: 9.8 us -> 9.83 us
  transfers between devices with their start and end apart: 16 -> 22, of which waited for: 3 -> 9; matrix products, arithmetic and copies ran while one was open for 2% -> 1% of each run, Pallas kernels for 0% -> 0%
where the time goes in v1:
time: 302 us; the launch traced here: 300 us
  waiting for transfers between devices  148 us (49%)
  starting transfers between devices  54 us (18%)
  local copies, waits for them, and re-layouts  39.3 us (13%)
  other arithmetic  25.2 us (8%)
  matrix products  21.6 us (7%)
  blocking collectives  10.6 us (4%)
    ppermute x6, waiting for transfers between devices, sum_by_hops(): lax.ppermute(total, axis, [(i, i ^ hop) for i in range(size)])  139 us
    ppermute x8, starting transfers between devices, padded(): lax.ppermute(head, axis, [((i + 1) % count, i) for i in range(ends)])  24.6 us
    ppermute x8, starting transfers between devices, padded(): lax.ppermute(tail, axis, [(i, (i + 1) % count) for i in range(ends)])  21.6 us
    scatter-add x4, other arithmetic, apply_operator(): jnp.zeros(vector.shape, jnp.float32).at[flat_rows].add(coupling_terms)  18.5 us
    gather x4, local copies, waits for them, and re-layouts, neighbour_faces(): face_vals = vector_b[face_index]  10.6 us
    all_gather x2, blocking collectives, per_device(): lax.all_gather(restricted, 'col', axis=0, tiled=True)  10.6 us
    scatter-add x4, local copies, waits for them, and re-layouts, apply_operator(): jnp.zeros(vector.shape, jnp.float32).at[flat_rows].add(coupling_terms)  10.2 us
    unnamed x21, local copies, waits for them, and re-layouts  9.83 us
  transfers between devices with their start and end apart: 22, of which 9 were waited for; matrix products, arithmetic and copies ran while one was open for 1% of the time, Pallas kernels for 0%

profile of v1, /device:TPU:9, one launch (start us, length us, event | category | flops | bytes accessed | tf_op | source)
XLA Modules:
  0.0 299.9 jit_solution(9948670978928591235)
XLA Ops:
  2.3 6.1 %all_gather.6 = bf16[384,256]{1,0:T(8,128)(2,1)S(1)} all-gather(bf16[96,256]{1,0:T(8,128)(2,1)S(1)} %convolution_convert_fusion), channel_id=1, replica_groups=mesh['row'=8,'col'=4] {'col'}, dimensions={0}, use_global_device_ids=true | all-gather | bytes 245760 | tf_op jit(solution)/shard_map/all_gather | solution.py:67
  11.2 17.7 %collective-permute-done = f32[768,256]{0,1:T(8,128)S(1)} collective-permute-done((f32[768,256]{0,1:T(8,128)S(1)}, f32[768,256]{0,1:T(8,128)S(1)}, u32[]{:S(2)}, u32[]{:S(2)}) %collective-permute-start) | collective-permute-done | bytes 786464 | tf_op jit(solution)/shard_map/ppermute | solution.py:13
  29.1 18.1 %collective-permute-done.1 = f32[768,256]{0,1:T(8,128)S(1)} collective-permute-done((f32[768,256]{0,1:T(8,128)S(1)}, f32[768,256]{0,1:T(8,128)S(1)}, u32[]{:S(2)}, u32[]{:S(2)}) %collective-permute-start.1) | collective-permute-done | bytes 786464 | tf_op jit(solution)/shard_map/ppermute | solution.py:13
  49.7 34.0 %collective-permute-done.2 = f32[768,256]{0,1:T(8,128)} collective-permute-done((f32[768,256]{0,1:T(8,128)S(1)}, f32[768,256]{0,1:T(8,128)}, u32[]{:S(2)}, u32[]{:S(2)}) %collective-permute-start.2) | collective-permute-done | bytes 786464 | tf_op jit(solution)/shard_map/ppermute | solution.py:13
  88.8 3.1 %collective-permute-start.3 = (bf16[1,128,256]{2,1,0:T(8,128)(2,1)}, bf16[1,128,256]{2,1,0:T(8,128)(2,1)S(1)}, u32[]{:S(2)}, u32[]{:S(2)}) collective-permute-start(bf16[1,128,256]{2,1,0:T(8,128)(2,1)} %get-tuple-element.20), channel_id=1, source_target_pairs={{0,4},{4,8},{8,12},{12,16},{16,20},{20,24},{24,28},{1,5},{5,9},{9,... | collective-permute-start | bytes 196616 | tf_op jit(solution)/shard_map/ppermute | solution.py:26
  92.0 3.8 %collective-permute-start.5 = (bf16[1,128,256]{2,1,0:T(8,128)(2,1)}, bf16[1,128,256]{2,1,0:T(8,128)(2,1)}, u32[]{:S(2)}, u32[]{:S(2)}) collective-permute-start(bf16[1,128,256]{2,1,0:T(8,128)(2,1)} %get-tuple-element.21), channel_id=1, source_target_pairs={{0,1},{1,2},{2,3},{4,5},{5,6},{6,7},{8,9},{9,10},{10,11},{12,13},{... | collective-permute-start | bytes 196616 | tf_op jit(solution)/shard_map/ppermute | solution.py:26
  106.2 4.8 %scatter_custom_fusion = f32[1024,256]{1,0:T(8,128)} fusion(s32[512]{0:T(512)S(1)} %bitcast.127, bf16[512,256]{1,0:T(8,128)(2,1)} %bitcast.119, f32[]{:T(128)} %constant.4.clone.1, f32[512]{0:T(512)S(1)} %bitcast.122), kind=kCustom, calls=%fused_computation.40 | custom fusion | flops 393216 | bytes 1312772 | tf_op jit(solution)/shard_map/scatter-add | solution.py:52
  113.5 4.8 %convolution_add_fusion.2 = f32[256,1024]{1,0:T(8,128)} fusion(f32[256,1024]{1,0:T(8,128)} %copy-done.3, bf16[1024,1024]{1,0:T(8,128)(2,1)} %param.9, f32[1024,256]{0,1:T(8,128)S(1)} %copy.33, f32[1024,256]{0,1:T(8,128)} %copy.32, bf16[1024,1024]{1,0:T(8,128)(2,1)S(1)} %copy-done), kind=kOutput, calls=%fused_computation.23 | convolution fusion | flops 1075052544 | bytes 8388608 | tf_op jit(solution)/shard_map/dot_general | solution.py:79
  122.5 3.3 %gather_fusion.1 = bf16[512,256]{1,0:T(8,128)(2,1)} fusion(bf16[1024,256]{1,0:T(8,128)(2,1)} %copy.34, s32[1024]{0:T(1024)S(1)} %pad_clamp_fusion), kind=kCustom, calls=%fused_computation.1 | custom fusion | bytes 526336 | tf_op jit(solution)/shard_map/gather | solution.py:42
  131.0 3.9 %collective-permute-start.8 = (bf16[1,128,256]{2,1,0:T(8,128)(2,1)S(1)}, bf16[1,128,256]{2,1,0:T(8,128)(2,1)S(1)}, u32[]{:S(2)}, u32[]{:S(2)}) collective-permute-start(bf16[1,128,256]{2,1,0:T(8,128)(2,1)S(1)} %get-tuple-element.18), channel_id=1, source_target_pairs={{4,0},{8,4},{12,8},{16,12},{20,16},{24,20},{28,24},{5,1},{9,5},{13... | collective-permute-start | bytes 196616 | tf_op jit(solution)/shard_map/ppermute | solution.py:28
  141.3 4.8 %scatter_custom_fusion.1 = f32[1024,256]{1,0:T(8,128)} fusion(s32[512]{0:T(512)S(1)} %bitcast.128, bf16[512,256]{1,0:T(8,128)(2,1)} %bitcast.120, f32[]{:T(128)} %constant.4.clone.1, f32[512]{0:T(512)S(1)} %bitcast.123), kind=kCustom, calls=%fused_computation.38 | custom fusion | flops 393216 | bytes 1312772 | tf_op jit(solution)/shard_map/scatter-add | solution.py:52
  151.2 4.4 %all_gather.7 = bf16[384,256]{1,0:T(8,128)(2,1)S(1)} all-gather(bf16[96,256]{1,0:T(8,128)(2,1)S(1)} %fusion.14), channel_id=1, replica_groups=mesh['row'=8,'col'=4] {'col'}, dimensions={0}, use_global_device_ids=true | all-gather | bytes 245760 | tf_op jit(solution)/shard_map/all_gather | solution.py:67
  157.2 18.7 %collective-permute-done.11 = f32[768,256]{0,1:T(8,128)S(1)} collective-permute-done((f32[768,256]{0,1:T(8,128)S(1)}, f32[768,256]{0,1:T(8,128)S(1)}, u32[]{:S(2)}, u32[]{:S(2)}) %collective-permute-start.11) | collective-permute-done | bytes 786464 | tf_op jit(solution)/shard_map/ppermute | solution.py:13
  176.7 17.2 %collective-permute-done.12 = f32[768,256]{0,1:T(8,128)S(1)} collective-permute-done((f32[768,256]{0,1:T(8,128)S(1)}, f32[768,256]{0,1:T(8,128)S(1)}, u32[]{:S(2)}, u32[]{:S(2)}) %collective-permute-start.12) | collective-permute-done | bytes 786464 | tf_op jit(solution)/shard_map/ppermute | solution.py:13
  194.1 3.3 %collective-permute-start.13 = (f32[768,256]{0,1:T(8,128)S(1)}, f32[768,256]{0,1:T(8,128)S(1)}, u32[]{:S(2)}, u32[]{:S(2)}) collective-permute-start(f32[768,256]{0,1:T(8,128)S(1)} %add.78), channel_id=1, source_target_pairs={{0,16},{4,20},{8,24},{12,28},{16,0},{20,4},{24,8},{28,12},{1,17},{... | collective-permute-start | bytes 2359304 | tf_op jit(solution)/shard_map/ppermute | solution.py:13
  197.3 33.6 %collective-permute-done.13 = f32[768,256]{0,1:T(8,128)S(1)} collective-permute-done((f32[768,256]{0,1:T(8,128)S(1)}, f32[768,256]{0,1:T(8,128)S(1)}, u32[]{:S(2)}, u32[]{:S(2)}) %collective-permute-start.13) | collective-permute-done | bytes 786464 | tf_op jit(solution)/shard_map/ppermute | solution.py:13
  239.8 4.7 %collective-permute-start.16 = (bf16[1,128,256]{2,1,0:T(8,128)(2,1)S(1)}, bf16[1,128,256]{2,1,0:T(8,128)(2,1)S(1)}, u32[]{:S(2)}, u32[]{:S(2)}) collective-permute-start(bf16[1,128,256]{2,1,0:T(8,128)(2,1)S(1)} %get-tuple-element.13), channel_id=1, source_target_pairs={{0,1},{1,2},{2,3},{4,5},{5,6},{6,7},{8,9},{9,10},{10,11},{12,13},{... | collective-permute-start | bytes 196616 | tf_op jit(solution)/shard_map/ppermute | solution.py:26
  244.5 4.3 %collective-permute-start.15 = (bf16[1,128,256]{2,1,0:T(8,128)(2,1)S(1)}, bf16[1,128,256]{2,1,0:T(8,128)(2,1)S(1)}, u32[]{:S(2)}, u32[]{:S(2)}) collective-permute-start(bf16[1,128,256]{2,1,0:T(8,128)(2,1)S(1)} %get-tuple-element.14), channel_id=1, source_target_pairs={{4,0},{8,4},{12,8},{16,12},{20,16},{24,20},{28,24},{5,1},{9,5},{13... | collective-permute-start | bytes 196616 | tf_op jit(solution)/shard_map/ppermute | solution.py:28
  250.7 3.6 %collective-permute-done.17 = bf16[1,128,256]{2,1,0:T(8,128)(2,1)S(1)} collective-permute-done((bf16[1,128,256]{2,1,0:T(8,128)(2,1)S(1)}, bf16[1,128,256]{2,1,0:T(8,128)(2,1)S(1)}, u32[]{:S(2)}, u32[]{:S(2)}) %collective-permute-start.17) | collective-permute-done | bytes 65568 | tf_op jit(solution)/shard_map/ppermute | solution.py:28
  254.4 4.4 %scatter_custom_fusion.2 = f32[1024,256]{1,0:T(8,128)} fusion(s32[512]{0:T(512)S(1)} %bitcast.129, bf16[512,256]{1,0:T(8,128)(2,1)S(1)} %bitcast.121, f32[]{:T(128)} %constant.4.clone.1, f32[512]{0:T(512)S(1)} %bitcast.124), kind=kCustom, calls=%fused_computation.36 | custom fusion | flops 393216 | bytes 1312772 | tf_op jit(solution)/shard_map/scatter-add | solution.py:52
  261.3 5.0 %fusion.42 = (bf16[1024,256]{0,1:T(8,128)(2,1)}, f32[1024,256]{0,1:T(8,128)}) fusion(f32[256,1024]{1,0:T(8,128)} %copy-done.1, bf16[1024,1024]{1,0:T(8,128)(2,1)} %param.9, f32[1024,256]{0,1:T(8,128)S(1)} %copy.33, f32[1024,256]{0,1:T(8,128)} %copy.38, bf16[1024,1024]{1,0:T(8,128)(2,1)S(1)} %copy-done), kind=kOutput, calls=%fused_computation.87 | convolution fusion | flops 1075314688 | bytes 8912896 | tf_op jit(solution)/shard_map/dot_general | solution.py:79
  275.5 4.5 %collective-permute-start.19 = (bf16[1,128,256]{2,1,0:T(8,128)(2,1)}, bf16[1,128,256]{2,1,0:T(8,128)(2,1)S(1)}, u32[]{:S(2)}, u32[]{:S(2)}) collective-permute-start(bf16[1,128,256]{2,1,0:T(8,128)(2,1)} %get-tuple-element.10), channel_id=1, source_target_pairs={{4,0},{8,4},{12,8},{16,12},{20,16},{24,20},{28,24},{5,1},{9,5},{13... | collective-permute-start | bytes 196616 | tf_op jit(solution)/shard_map/ppermute | solution.py:28
  287.2 4.4 %scatter_custom_fusion.3 = f32[1024,256]{1,0:T(8,128)} fusion(s32[512]{0:T(512)S(1)} %bitcast.130, bf16[512,256]{1,0:T(8,128)(2,1)S(1)} %bitcast.118, f32[]{:T(128)} %constant.4.clone.1, f32[512]{0:T(512)S(1)} %bitcast.125), kind=kCustom, calls=%fused_computation.34 | custom fusion | flops 393216 | bytes 1312772 | tf_op jit(solution)/shard_map/scatter-add | solution.py:52
  294.2 3.1 %fusion.7 = f32[1024,256]{0,1:T(8,128)} fusion(f32[1024,256]{0,1:T(8,128)S(1)} %copy.33, f32[1024,256]{0,1:T(8,128)} %copy.41, bf16[1024,256]{0,1:T(8,128)(2,1)} %get-tuple-element.24, bf16[1024,1024]{1,0:T(8,128)(2,1)S(1)} %copy-done), kind=kOutput, calls=%fused_computation.20 | convolution fusion | flops 537395200 | bytes 5767168 | tf_op jit(solution)/shard_map/dot_general | solution.py:53
  (86 shorter events, 83.2 us)
Async XLA Ops:
  0.6 112.9 %copy-start = (bf16[1024,1024]{1,0:T(8,128)(2,1)S(1)}, bf16[1024,1024]{1,0:T(8,128)(2,1)}, u32[]{:S(2)}) copy-start(bf16[1024,1024]{1,0:T(8,128)(2,1)} %param.8) | copy-start | bytes 6291460
  9.9 19.0 %collective-permute-start = (f32[768,256]{0,1:T(8,128)S(1)}, f32[768,256]{0,1:T(8,128)S(1)}, u32[]{:S(2)}, u32[]{:S(2)}) collective-permute-start(f32[768,256]{0,1:T(8,128)S(1)} %convolution_bitcast_fusion.5), channel_id=1, source_target_pairs={{0,4},{4,0},{8,12},{12,8},{16,20},{20,16},{24,28},{28,24},{1,5},{5... | collective-permute-start | bytes 2359304 | tf_op jit(solution)/shard_map/ppermute | solution.py:13
  29.0 18.1 %collective-permute-start.1 = (f32[768,256]{0,1:T(8,128)S(1)}, f32[768,256]{0,1:T(8,128)S(1)}, u32[]{:S(2)}, u32[]{:S(2)}) collective-permute-start(f32[768,256]{0,1:T(8,128)S(1)} %add.70), channel_id=1, source_target_pairs={{0,8},{4,12},{8,0},{12,4},{16,24},{20,28},{24,16},{28,20},{1,9},{5... | collective-permute-start | bytes 2359304 | tf_op jit(solution)/shard_map/ppermute | solution.py:13
  47.3 36.4 %collective-permute-start.2 = (f32[768,256]{0,1:T(8,128)S(1)}, f32[768,256]{0,1:T(8,128)}, u32[]{:S(2)}, u32[]{:S(2)}) collective-permute-start(f32[768,256]{0,1:T(8,128)S(1)} %add.71), channel_id=1, source_target_pairs={{0,16},{4,20},{8,24},{12,28},{16,0},{20,4},{24,8},{28,12},{1,17},{... | collective-permute-start | bytes 2359304 | tf_op jit(solution)/shard_map/ppermute | solution.py:13
  88.8 13.5 %collective-permute-start.3 = (bf16[1,128,256]{2,1,0:T(8,128)(2,1)}, bf16[1,128,256]{2,1,0:T(8,128)(2,1)S(1)}, u32[]{:S(2)}, u32[]{:S(2)}) collective-permute-start(bf16[1,128,256]{2,1,0:T(8,128)(2,1)} %get-tuple-element.20), channel_id=1, source_target_pairs={{0,4},{4,8},{8,12},{12,16},{16,20},{20,24},{24,28},{1,5},{5,9},{9,... | collective-permute-start | bytes 196616 | tf_op jit(solution)/shard_map/ppermute | solution.py:26
  92.0 10.4 %collective-permute-start.5 = (bf16[1,128,256]{2,1,0:T(8,128)(2,1)}, bf16[1,128,256]{2,1,0:T(8,128)(2,1)}, u32[]{:S(2)}, u32[]{:S(2)}) collective-permute-start(bf16[1,128,256]{2,1,0:T(8,128)(2,1)} %get-tuple-element.21), channel_id=1, source_target_pairs={{0,1},{1,2},{2,3},{4,5},{5,6},{6,7},{8,9},{9,10},{10,11},{12,13},{... | collective-permute-start | bytes 196616 | tf_op jit(solution)/shard_map/ppermute | solution.py:26
  95.8 6.6 %collective-permute-start.4 = (bf16[1,128,256]{2,1,0:T(8,128)(2,1)S(1)}, bf16[1,128,256]{2,1,0:T(8,128)(2,1)}, u32[]{:S(2)}, u32[]{:S(2)}) collective-permute-start(bf16[1,128,256]{2,1,0:T(8,128)(2,1)S(1)} %get-tuple-element.22), channel_id=1, source_target_pairs={{4,0},{8,4},{12,8},{16,12},{20,16},{24,20},{28,24},{5,1},{9,5},{13... | collective-permute-start | bytes 196616 | tf_op jit(solution)/shard_map/ppermute | solution.py:28
  98.8 5.7 %collective-permute-start.6 = (bf16[1,128,256]{2,1,0:T(8,128)(2,1)S(1)}, bf16[1,128,256]{2,1,0:T(8,128)(2,1)}, u32[]{:S(2)}, u32[]{:S(2)}) collective-permute-start(bf16[1,128,256]{2,1,0:T(8,128)(2,1)S(1)} %get-tuple-element.23), channel_id=1, source_target_pairs={{1,0},{2,1},{3,2},{5,4},{6,5},{7,6},{9,8},{10,9},{11,10},{13,12},{... | collective-permute-start | bytes 196616 | tf_op jit(solution)/shard_map/ppermute | solution.py:28
  126.7 10.8 %collective-permute-start.7 = (bf16[1,128,256]{2,1,0:T(8,128)(2,1)S(1)}, bf16[1,128,256]{2,1,0:T(8,128)(2,1)S(1)}, u32[]{:S(2)}, u32[]{:S(2)}) collective-permute-start(bf16[1,128,256]{2,1,0:T(8,128)(2,1)S(1)} %get-tuple-element.16), channel_id=1, source_target_pairs={{0,4},{4,8},{8,12},{12,16},{16,20},{20,24},{24,28},{1,5},{5,9},{9,... | collective-permute-start | bytes 196616 | tf_op jit(solution)/shard_map/ppermute | solution.py:26
  128.9 8.6 %collective-permute-start.9 = (bf16[1,128,256]{2,1,0:T(8,128)(2,1)S(1)}, bf16[1,128,256]{2,1,0:T(8,128)(2,1)S(1)}, u32[]{:S(2)}, u32[]{:S(2)}) collective-permute-start(bf16[1,128,256]{2,1,0:T(8,128)(2,1)S(1)} %get-tuple-element.17), channel_id=1, source_target_pairs={{0,1},{1,2},{2,3},{4,5},{5,6},{6,7},{8,9},{9,10},{10,11},{12,13},{... | collective-permute-start | bytes 196616 | tf_op jit(solution)/shard_map/ppermute | solution.py:26
  131.0 6.6 %collective-permute-start.8 = (bf16[1,128,256]{2,1,0:T(8,128)(2,1)S(1)}, bf16[1,128,256]{2,1,0:T(8,128)(2,1)S(1)}, u32[]{:S(2)}, u32[]{:S(2)}) collective-permute-start(bf16[1,128,256]{2,1,0:T(8,128)(2,1)S(1)} %get-tuple-element.18), channel_id=1, source_target_pairs={{4,0},{8,4},{12,8},{16,12},{20,16},{24,20},{28,24},{5,1},{9,5},{13... | collective-permute-start | bytes 196616 | tf_op jit(solution)/shard_map/ppermute | solution.py:28
  135.0 5.6 %collective-permute-start.10 = (bf16[1,128,256]{2,1,0:T(8,128)(2,1)S(1)}, bf16[1,128,256]{2,1,0:T(8,128)(2,1)S(1)}, u32[]{:S(2)}, u32[]{:S(2)}) collective-permute-start(bf16[1,128,256]{2,1,0:T(8,128)(2,1)S(1)} %get-tuple-element.19), channel_id=1, source_target_pairs={{1,0},{2,1},{3,2},{5,4},{6,5},{7,6},{9,8},{10,9},{11,10},{13,12},{... | collective-permute-start | bytes 196616 | tf_op jit(solution)/shard_map/ppermute | solution.py:28
  157.1 73.8 %copy-start.2 = (f32[256,1024]{1,0:T(8,128)S(1)}, f32[256,1024]{1,0:T(8,128)}, u32[]{:S(2)}) copy-start(f32[256,1024]{1,0:T(8,128)} %convolution_add_fusion.2) | copy-start | bytes 3145732
  157.1 18.8 %collective-permute-start.11 = (f32[768,256]{0,1:T(8,128)S(1)}, f32[768,256]{0,1:T(8,128)S(1)}, u32[]{:S(2)}, u32[]{:S(2)}) collective-permute-start(f32[768,256]{0,1:T(8,128)S(1)} %convolution_bitcast_fusion.4), channel_id=1, source_target_pairs={{0,4},{4,0},{8,12},{12,8},{16,20},{20,16},{24,28},{28,24},{1,5},{5... | collective-permute-start | bytes 2359304 | tf_op jit(solution)/shard_map/ppermute | solution.py:13
  176.0 18.0 %collective-permute-start.12 = (f32[768,256]{0,1:T(8,128)S(1)}, f32[768,256]{0,1:T(8,128)S(1)}, u32[]{:S(2)}, u32[]{:S(2)}) collective-permute-start(f32[768,256]{0,1:T(8,128)S(1)} %add.77), channel_id=1, source_target_pairs={{0,8},{4,12},{8,0},{12,4},{16,24},{20,28},{24,16},{28,20},{1,9},{5... | collective-permute-start | bytes 2359304 | tf_op jit(solution)/shard_map/ppermute | solution.py:13
  194.1 36.8 %collective-permute-start.13 = (f32[768,256]{0,1:T(8,128)S(1)}, f32[768,256]{0,1:T(8,128)S(1)}, u32[]{:S(2)}, u32[]{:S(2)}) collective-permute-start(f32[768,256]{0,1:T(8,128)S(1)} %add.78), channel_id=1, source_target_pairs={{0,16},{4,20},{8,24},{12,28},{16,0},{20,4},{24,8},{28,12},{1,17},{... | collective-permute-start | bytes 2359304 | tf_op jit(solution)/shard_map/ppermute | solution.py:13
  237.9 12.8 %collective-permute-start.14 = (bf16[1,128,256]{2,1,0:T(8,128)(2,1)S(1)}, bf16[1,128,256]{2,1,0:T(8,128)(2,1)S(1)}, u32[]{:S(2)}, u32[]{:S(2)}) collective-permute-start(bf16[1,128,256]{2,1,0:T(8,128)(2,1)S(1)} %get-tuple-element.12), channel_id=1, source_target_pairs={{0,4},{4,8},{8,12},{12,16},{16,20},{20,24},{24,28},{1,5},{5,9},{9,... | collective-permute-start | bytes 196616 | tf_op jit(solution)/shard_map/ppermute | solution.py:26
  239.8 10.9 %collective-permute-start.16 = (bf16[1,128,256]{2,1,0:T(8,128)(2,1)S(1)}, bf16[1,128,256]{2,1,0:T(8,128)(2,1)S(1)}, u32[]{:S(2)}, u32[]{:S(2)}) collective-permute-start(bf16[1,128,256]{2,1,0:T(8,128)(2,1)S(1)} %get-tuple-element.13), channel_id=1, source_target_pairs={{0,1},{1,2},{2,3},{4,5},{5,6},{6,7},{8,9},{9,10},{10,11},{12,13},{... | collective-permute-start | bytes 196616 | tf_op jit(solution)/shard_map/ppermute | solution.py:26
  244.5 6.2 %collective-permute-start.15 = (bf16[1,128,256]{2,1,0:T(8,128)(2,1)S(1)}, bf16[1,128,256]{2,1,0:T(8,128)(2,1)S(1)}, u32[]{:S(2)}, u32[]{:S(2)}) collective-permute-start(bf16[1,128,256]{2,1,0:T(8,128)(2,1)S(1)} %get-tuple-element.14), channel_id=1, source_target_pairs={{4,0},{8,4},{12,8},{16,12},{20,16},{24,20},{28,24},{5,1},{9,5},{13... | collective-permute-start | bytes 196616 | tf_op jit(solution)/shard_map/ppermute | solution.py:28
  248.7 5.6 %collective-permute-start.17 = (bf16[1,128,256]{2,1,0:T(8,128)(2,1)S(1)}, bf16[1,128,256]{2,1,0:T(8,128)(2,1)S(1)}, u32[]{:S(2)}, u32[]{:S(2)}) collective-permute-start(bf16[1,128,256]{2,1,0:T(8,128)(2,1)S(1)} %get-tuple-element.15), channel_id=1, source_target_pairs={{1,0},{2,1},{3,2},{5,4},{6,5},{7,6},{9,8},{10,9},{11,10},{13,12},{... | collective-permute-start | bytes 196616 | tf_op jit(solution)/shard_map/ppermute | solution.py:28
  271.7 13.3 %collective-permute-start.18 = (bf16[1,128,256]{2,1,0:T(8,128)(2,1)}, bf16[1,128,256]{2,1,0:T(8,128)(2,1)S(1)}, u32[]{:S(2)}, u32[]{:S(2)}) collective-permute-start(bf16[1,128,256]{2,1,0:T(8,128)(2,1)} %get-tuple-element.8), channel_id=1, source_target_pairs={{0,4},{4,8},{8,12},{12,16},{16,20},{20,24},{24,28},{1,5},{5,9},{9,... | collective-permute-start | bytes 196616 | tf_op jit(solution)/shard_map/ppermute | solution.py:26
  273.6 11.4 %collective-permute-start.20 = (bf16[1,128,256]{2,1,0:T(8,128)(2,1)}, bf16[1,128,256]{2,1,0:T(8,128)(2,1)S(1)}, u32[]{:S(2)}, u32[]{:S(2)}) collective-permute-start(bf16[1,128,256]{2,1,0:T(8,128)(2,1)} %get-tuple-element.9), channel_id=1, source_target_pairs={{0,1},{1,2},{2,3},{4,5},{5,6},{6,7},{8,9},{9,10},{10,11},{12,13},{... | collective-permute-start | bytes 196616 | tf_op jit(solution)/shard_map/ppermute | solution.py:26
  275.5 9.5 %collective-permute-start.19 = (bf16[1,128,256]{2,1,0:T(8,128)(2,1)}, bf16[1,128,256]{2,1,0:T(8,128)(2,1)S(1)}, u32[]{:S(2)}, u32[]{:S(2)}) collective-permute-start(bf16[1,128,256]{2,1,0:T(8,128)(2,1)} %get-tuple-element.10), channel_id=1, source_target_pairs={{4,0},{8,4},{12,8},{16,12},{20,16},{24,20},{28,24},{5,1},{9,5},{13... | collective-permute-start | bytes 196616 | tf_op jit(solution)/shard_map/ppermute | solution.py:28
  280.0 6.3 %collective-permute-start.21 = (bf16[1,128,256]{2,1,0:T(8,128)(2,1)S(1)}, bf16[1,128,256]{2,1,0:T(8,128)(2,1)}, u32[]{:S(2)}, u32[]{:S(2)}) collective-permute-start(bf16[1,128,256]{2,1,0:T(8,128)(2,1)S(1)} %get-tuple-element.11), channel_id=1, source_target_pairs={{1,0},{2,1},{3,2},{5,4},{6,5},{7,6},{9,8},{10,9},{11,10},{13,12},{... | collective-permute-start | bytes 196616 | tf_op jit(solution)/shard_map/ppermute | solution.py:28
  (7 other events, 134.6 us)
